TPU v7x, 32 devices: a whole 2x2x4 slice. The times are simulated.
32 devices in a mesh: gx: 2 (over core), gy: 8 (over z, y), gz: 2 (over x).
Axes of the slice: x: 2, y: 2, z: 4, core: 2. Of those that a mesh axis runs over, the one named last changes fastest.
Arguments:
- number_densities: float32 [64, 8, 32, 256], P(None, 'gx', 'gy', 'gz'), may hold values from 0.0125 to 24, as said below
- kinetic_kelvin: float32 [8, 32, 256], P('gx', 'gy', 'gz'), may hold values from 0.5 to 3
- flow_vector: float32 [3, 8, 32, 256], P(None, 'gx', 'gy', 'gz'), may hold values from -1 to 1
- opacity_area: float32 [128, 64], replicated, may hold values from 0.0078125 to 0.078125
- illumination: float32 [6], replicated, may hold values from 0.2 to 1
- arrhenius_coefficient: float32 [128], replicated, may hold values from 0.1 to 1
- arrhenius_barrier: float32 [128], replicated, may hold values from 0.5 to 5
- exothermic_energy: float32 [256], replicated, may hold values from 0.002 to 0.02
- emission_loss: float32 [64], replicated, may hold values from 0.01 to 0.1
- participant_indices: int32 [4, 256], replicated, may hold values from 0 to 63
- demanding_patches: int32 [2, 8, 2, 4], P('gx', 'gy', 'gz'), may hold values from 0 to 16, as said below
Outputs:
- ending_populations: float32 [64, 8, 32, 256], P(None, 'gx', 'gy', 'gz')
- ending_warmth: float32 [8, 32, 256], P('gx', 'gy', 'gz')
Inputs may be any that keep to these rules, and one draw needn't show every extreme that they name: `participant_indices`: stoichiometry names species. `number_densities`: densities are positive. `demanding_patches`: each brick's row holds distinct tile numbers first and 16 in its remaining slots; a brick lists at most 4 tiles and some brick lists exactly 4; the 2 bricks that share their first two brick indices together list exactly 4 tiles.
All inputs are finite; a program needn't handle non-finite values.
Results may differ from a plain program's by a relative error of at most 0.0003.
Values sent between devices are 32-bit elements; how exact they have to be, the bound alone decides.
A program may use at most 64 MiB of HBM per device.

v0:
```python
import functools

import jax
import jax.numpy as jnp
from jax import lax
from jax.experimental import pallas as pl
from jax.experimental.pallas import tpu as pltpu
from jax.sharding import PartitionSpec as P

NSUB = 8
COURANT = 0.25
MESH = pl.DeviceIdType.MESH
F32 = jnp.float32
BF16 = jnp.bfloat16


def halves(x):
    high = x.astype(BF16)
    return high, (x - high.astype(F32)).astype(BF16)


def stacked(x):
    high, low = halves(x)
    return jnp.concatenate([high, low], axis=0)


def dot(a, b):
    return jnp.dot(a, b, preferred_element_type=F32)


def kernel(
    sizes,
    extents,
    n_ref,
    t_ref,
    flow_ref,
    opacity_ref,
    coef_ref,
    barrier_ref,
    energy_ref,
    emission_ref,
    part_ref,
    illum_ref,
    patch_ref,
    out_ref,
    warm_ref,
    tiles,
    depth,
    photo,
    chem,
    acc,
    xsum,
    xother,
    zsum,
    zother,
    scan,
    scan_in,
    below,
    flow_x,
    flow_l,
    flow_r,
    flow_z,
    halo_x,
    halo_l,
    halo_r,
    zpack,
    halo_z,
    hard_n,
    hard_t,
    op_hi,
    op_lo,
    pick,
    gather_mat,
    tally_mat,
    tri,
    coef_b,
    barr_b,
    sem_first_s,
    sem_first_r,
    sem_scan_s,
    sem_scan_r,
    sem_x_s,
    sem_x_r,
    sem_l_s,
    sem_l_r,
    sem_rt_s,
    sem_rt_r,
    sem_z_s,
    sem_z_r,
):
    kinds, east, north, lanes, photons, reactions, slots, ngy, levels = sizes
    patches = east * north
    gx, gy, gz = lax.axis_index("gx"), lax.axis_index("gy"), lax.axis_index("gz")
    peer_x = (1 - gx, gy, gz)
    peer_z = (gx, gy, 1 - gz)
    left = (gx, lax.rem(gy + ngy - 1, ngy), gz)
    right = (gx, lax.rem(gy + 1, ngy), gz)
    bits = [lax.rem(gy // (1 << k), 2) for k in range(levels)]
    partners = [(gx, gy + (1 << k) * (1 - 2 * bits[k]), gz) for k in range(levels)]

    entry = pltpu.get_barrier_semaphore()
    peers = [peer_x, peer_z, left, right] + partners
    for peer in peers:
        pl.semaphore_signal(entry, inc=1, device_id=peer, device_id_type=MESH)

    def send(src, dst, ssem, rsem, to):
        return pltpu.make_async_remote_copy(
            src_ref=src,
            dst_ref=dst,
            send_sem=ssem,
            recv_sem=rsem,
            device_id=to,
            device_id_type=MESH,
        )

    lane = lax.broadcasted_iota(jnp.int32, (kinds, lanes), 1)

    xs = [None] * north
    zt = jnp.zeros((kinds, lanes), F32)
    for i in range(east):
        row = None
        for j in range(north):
            t = i * north + j
            v = n_ref[pl.ds(t, kinds, stride=patches), :]
            tiles[t] = v
            row = v if row is None else row + v
            xs[j] = v if xs[j] is None else xs[j] + v
            zt = jnp.where(lane == t, jnp.sum(v, axis=1, keepdims=True), zt)
        scan[0, i] = row
    for j in range(north):
        xsum[j] = xs[j]
    zsum[...] = zt

    pl.semaphore_wait(entry, len(peers))

    def scan_copy(k, i):
        return send(
            scan.at[k, i], scan_in.at[k, i], sem_scan_s.at[k, i], sem_scan_r.at[k, i], partners[k]
        )

    for i in range(east):
        scan_copy(0, i).start()
    first = [
        send(xsum, xother, sem_first_s.at[0], sem_first_r.at[0], peer_x),
        send(zsum, zother, sem_first_s.at[1], sem_first_r.at[1], peer_z),
        send(
            flow_ref.at[pl.ds(0, patches)], flow_x, sem_first_s.at[2], sem_first_r.at[2], peer_x
        ),
        send(
            flow_ref.at[pl.ds(patches, patches)],
            flow_r,
            sem_first_s.at[3],
            sem_first_r.at[3],
            left,
        ),
        send(
            flow_ref.at[pl.ds(patches, patches)],
            flow_l,
            sem_first_s.at[4],
            sem_first_r.at[4],
            right,
        ),
        send(
            flow_ref.at[pl.ds(2 * patches, patches)],
            flow_z,
            sem_first_s.at[5],
            sem_first_r.at[5],
            peer_z,
        ),
    ]
    for copy in first:
        copy.start()

    op = opacity_ref[...]
    op_high, op_low = halves(op)
    op_hi[...] = op_high
    lane_p = lax.broadcasted_iota(jnp.int32, op.shape, 1)
    op_lo[...] = jnp.where(lane_p < kinds, op_low.astype(F32), 0.0).astype(BF16)

    twice = lax.broadcasted_iota(jnp.int32, (2 * kinds, reactions), 0)
    twice = jnp.where(twice >= kinds, twice - kinds, twice)
    hot_a = (twice == part_ref[0:1, :]).astype(F32)
    gather_mat[0:reactions, :] = hot_a.T.astype(BF16)
    two = reactions - photons
    hot_b = (twice[:, photons:] == part_ref[1:2, photons:]).astype(F32)
    gather_mat[reactions : reactions + two, :] = hot_b.T.astype(BF16)
    extra = lax.broadcasted_iota(jnp.int32, (16, 2 * kinds), 0)
    q_high, q_low = halves(emission_ref[...])
    gather_mat[reactions + two :, :] = jnp.where(
        extra == 0, q_high.astype(F32), jnp.where(extra == 1, q_low.astype(F32), 0.0)
    ).astype(BF16)

    species = lax.broadcasted_iota(jnp.int32, (kinds, reactions), 0)
    which = lax.broadcasted_iota(jnp.int32, (kinds, reactions), 1)
    tally_mat[0:kinds, :] = (
        (species == part_ref[2:3, :]).astype(F32) + (species == part_ref[3:4, :]).astype(F32)
    ).astype(BF16)
    tally_mat[kinds : 2 * kinds, :] = (
        (species == part_ref[0:1, :]).astype(F32)
        + jnp.where(which >= photons, (species == part_ref[1:2, :]).astype(F32), 0.0)
    ).astype(BF16)
    extra = lax.broadcasted_iota(jnp.int32, (16, reactions), 0)
    e_high, e_low = halves(energy_ref[...])
    tally_mat[2 * kinds :, :] = jnp.where(
        extra == 0, e_high.astype(F32), jnp.where(extra == 1, e_low.astype(F32), 0.0)
    ).astype(BF16)

    source = lax.broadcasted_iota(jnp.int32, (2 * lanes, 2 * lanes), 0)
    source = jnp.where(source >= lanes, source - lanes, source)
    target = lax.broadcasted_iota(jnp.int32, (2 * lanes, 2 * lanes), 1)
    tri[...] = jnp.where(
        source < target, 1.0, jnp.where(source == target, 0.5, 0.0)
    ).astype(BF16)

    coef_b[...] = jnp.broadcast_to(coef_ref[...], (lanes, two)).T
    barr_b[...] = jnp.broadcast_to(-barrier_ref[...], (lanes, two)).T

    def project(x):
        s = stacked(x)
        return dot(op_hi[...], s) + dot(op_lo[...], s)

    def depth_row(i, carry):
        x = jnp.concatenate([tiles[i * north + j] for j in range(north)], axis=1)
        m = project(x)
        for j in range(north):
            depth[i * north + j] = m[:, j * lanes : (j + 1) * lanes]
        return carry

    lax.fori_loop(0, east, depth_row, 0)

    def scan_level(k):
        bit = bits[k].astype(F32)

        def chunk(i, carry):
            scan_copy(k, i).wait_recv()
            got = scan_in[k, i]
            scan[k + 1, i] = scan[k, i] + got
            if k == 0:
                below[i] = bit * got
            else:
                below[i] = below[i] + bit * got
            if k + 1 < levels:
                scan_copy(k + 1, i).start()
            return carry

        lax.fori_loop(0, east, chunk, 0)

    scan_level(0)

    first[0].wait_recv()
    high_x = gx.astype(F32)

    def x_lines(j, carry):
        other = project(xother[j])
        ms = [depth[i * north + j] for i in range(east)]
        whole = other
        for m in ms:
            whole = whole + m
        run = high_x * other
        for i in range(east):
            low = run + 0.5 * ms[i]
            up = whole - low
            photo[i * north + j] = illum_ref[0] * jnp.exp(
                low * (-1.0 / extents[0])
            ) + illum_ref[1] * jnp.exp(up * (-1.0 / extents[0]))
            run = run + ms[i]
        return carry

    lax.fori_loop(0, north, x_lines, 0)
    if levels > 1:
        scan_level(1)

    first[1].wait_recv()
    pick[...] = project(zother[...])
    high_z = gz.astype(F32)
    lane_r = lax.broadcasted_iota(jnp.int32, (photons, lanes), 1)

    def z_tile(t, carry):
        high, low_part = halves(depth[t])
        both = dot(jnp.concatenate([high, low_part], axis=1), tri[...])
        other = jnp.sum(jnp.where(lane_r == t, pick[...], 0.0), axis=1, keepdims=True)
        low = both[:, :lanes] + high_z * other
        up = both[:, lanes:] + other - low
        photo[t] = photo[t] + (
            illum_ref[4] * jnp.exp(low * (-1.0 / extents[2]))
            + illum_ref[5] * jnp.exp(up * (-1.0 / extents[2]))
        )
        return carry

    lax.fori_loop(0, patches, z_tile, 0)
    for k in range(2, levels):
        scan_level(k)

    def y_lines(i, carry):
        run = project(below[i])
        whole = project(scan[levels, i])
        for j in range(north):
            t = i * north + j
            low = run + 0.5 * depth[t]
            up = whole - low
            photo[t] = photo[t] + (
                illum_ref[2] * jnp.exp(low * (-1.0 / extents[1]))
                + illum_ref[3] * jnp.exp(up * (-1.0 / extents[1]))
            )
            run = run + depth[t]
        return carry

    lax.fori_loop(0, east, y_lines, 0)

    def react(ns, ts, ps, h):
        count = len(ns)
        g = dot(gather_mat[...], jnp.concatenate([stacked(n) for n in ns], axis=1))
        rates = []
        for q in range(count):
            c = slice(q * lanes, (q + 1) * lanes)
            speed = coef_b[...] * jnp.exp(barr_b[...] * (1.0 / ts[q]))
            rates.append(
                halves(
                    jnp.concatenate(
                        [
                            ps[q] * g[:photons, c],
                            speed * g[photons:reactions, c] * g[reactions : reactions + two, c],
                        ],
                        axis=0,
                    )
                )
            )
        pc = dot(tally_mat[...], jnp.concatenate([r[0] for r in rates], axis=1)) + dot(
            tally_mat[...], jnp.concatenate([r[1] for r in rates], axis=1)
        )
        new_n, new_t = [], []
        for q in range(count):
            c = slice(q * lanes, (q + 1) * lanes)
            n = ns[q]
            gained, used = pc[:kinds, c], pc[kinds : 2 * kinds, c]
            new_n.append((n + h * gained) * (n / (n + h * used)))
            heat = pc[2 * kinds : 2 * kinds + 1, c] + pc[2 * kinds + 1 : 2 * kinds + 2, c]
            cool = (
                g[reactions + two : reactions + two + 1, c]
                + g[reactions + two + 1 : reactions + two + 2, c]
            )
            new_t.append((ts[q] + h * heat) / (1.0 + h * cool))
        return new_n, new_t

    listed = [patch_ref[d] for d in range(slots)]
    chosen = [jnp.minimum(d, patches - 1) for d in listed]
    for d in range(slots):
        hard_n[d] = tiles[chosen[d]]
        hard_t[pl.ds(d, 1), :] = t_ref[pl.ds(chosen[d], 1), :]

    def substep(_, carry):
        ns = [hard_n[d] for d in range(slots)]
        ts = [hard_t[pl.ds(d, 1), :] for d in range(slots)]
        ps = [photo[chosen[d]] for d in range(slots)]
        ns, ts = react(ns, ts, ps, 1.0 / NSUB)
        for d in range(slots):
            hard_n[d] = ns[d]
            hard_t[pl.ds(d, 1), :] = ts[d]
        return carry

    lax.fori_loop(0, NSUB, substep, 0)

    def copy_left(i):
        return send(
            chem.at[pl.ds(i * north, 2)],
            halo_r.at[pl.ds(i * 2, 2)],
            sem_l_s.at[i],
            sem_l_r.at[i],
            left,
        )

    def copy_right(i):
        return send(
            chem.at[pl.ds(i * north + north - 2, 2)],
            halo_l.at[pl.ds(i * 2, 2)],
            sem_rt_s.at[i],
            sem_rt_r.at[i],
            right,
        )

    def copy_x(i):
        return send(
            chem.at[pl.ds(i * north, north)],
            halo_x.at[pl.ds(i * north, north)],
            sem_x_s.at[i],
            sem_x_r.at[i],
            peer_x,
        )

    def quiet_row(i, carry):
        index = [i * north + j for j in range(north)]
        ns = [tiles[t] for t in index]
        ts = [t_ref[pl.ds(t, 1), :] for t in index]
        ps = [photo[t] for t in index]
        ns, ts = react(ns, ts, ps, 1.0)
        for j in range(north):
            t = index[j]
            n, warm = ns[j], ts[j]
            for d in range(slots):
                n = jnp.where(jnp.full((kinds, lanes), listed[d] - t, jnp.int32) == 0, hard_n[d], n)
                warm = jnp.where(
                    jnp.full((1, lanes), listed[d] - t, jnp.int32) == 0,
                    hard_t[pl.ds(d, 1), :],
                    warm,
                )
            chem[t] = n
            warm_ref[pl.ds(t, 1), :] = warm
        copy_left(i).start()
        copy_right(i).start()
        copy_x(i).start()
        return carry

    lax.fori_loop(0, east, quiet_row, 0)

    packed = jnp.zeros((kinds, lanes), F32)
    for t in range(patches):
        rolled = pltpu.roll(chem[t], (4 * t + 2) % lanes, 1)
        packed = jnp.where(lane // 4 == t, rolled, packed)
    zpack[...] = packed
    zcopy = send(zpack, halo_z, sem_z_s.at[0], sem_z_r.at[0], peer_z)
    zcopy.start()

    for copy in first[2:]:
        copy.wait_recv()

    def flux(face, behind2, behind, ahead, ahead2):
        return face * jnp.where(
            face > 0, 1.5 * behind - 0.5 * behind2, 1.5 * ahead - 0.5 * ahead2
        )

    def flow_row(ref, t):
        return ref[pl.ds(t, 1), :]

    for i in range(east):
        copy_x(i).wait_recv()

    def advect_x(j, carry):
        cells = [halo_x[(east - 2) * north + j], halo_x[(east - 1) * north + j]]
        cells += [chem[i * north + j] for i in range(east)]
        cells += [halo_x[j], halo_x[north + j]]
        speed = [flow_row(flow_x, (east - 1) * north + j)]
        speed += [flow_row(flow_ref, i * north + j) for i in range(east)]
        speed += [flow_row(flow_x, j)]
        before = None
        for f in range(east + 1):
            face = jnp.broadcast_to(0.5 * (speed[f] + speed[f + 1]), (kinds, lanes))
            now = flux(face, cells[f], cells[f + 1], cells[f + 2], cells[f + 3])
            if f > 0:
                acc[(f - 1) * north + j] = now - before
            before = now
        return carry

    lax.fori_loop(0, north, advect_x, 0)

    zcopy.wait_recv()
    lane1 = lax.broadcasted_iota(jnp.int32, (1, lanes), 1)

    def roll(x, amount):
        return pltpu.roll(x, amount % lanes, 1)

    hz = halo_z[...]
    for t in range(patches):
        u = chem[t]
        b1 = jnp.where(lane == 0, roll(hz, -(4 * t + 1)), roll(u, 1))
        b2 = jnp.where(lane < 2, roll(hz, -4 * t), roll(u, 2))
        a1 = jnp.where(lane == lanes - 1, roll(hz, lanes - 1 - (4 * t + 2)), roll(u, -1))
        a2 = jnp.where(lane >= lanes - 2, roll(hz, lanes - 2 - (4 * t + 2)), roll(u, -2))
        v = flow_row(flow_ref, 2 * patches + t)
        vp = flow_row(flow_z, t)
        lower = 0.5 * (jnp.where(lane1 == 0, roll(vp, 1), roll(v, 1)) + v)
        upper = 0.5 * (v + jnp.where(lane1 == lanes - 1, roll(vp, -1), roll(v, -1)))
        lower = jnp.broadcast_to(lower, (kinds, lanes))
        upper = jnp.broadcast_to(upper, (kinds, lanes))
        acc[t] = acc[t] + (flux(upper, b1, u, a1, a2) - flux(lower, b2, b1, u, a1))

    for i in range(east):
        copy_left(i).wait_recv()
        copy_right(i).wait_recv()
        cells = [halo_l[2 * i], halo_l[2 * i + 1]]
        cells += [chem[i * north + j] for j in range(north)]
        cells += [halo_r[2 * i], halo_r[2 * i + 1]]
        speed = [flow_row(flow_l, i * north + north - 1)]
        speed += [flow_row(flow_ref, patches + i * north + j) for j in range(north)]
        speed += [flow_row(flow_r, i * north)]
        before = None
        for f in range(north + 1):
            face = jnp.broadcast_to(0.5 * (speed[f] + speed[f + 1]), (kinds, lanes))
            now = flux(face, cells[f], cells[f + 1], cells[f + 2], cells[f + 3])
            if f > 0:
                t = i * north + f - 1
                change = acc[t] + (now - before)
                out_ref[pl.ds(t, kinds, stride=patches), :] = chem[t] - COURANT * change
            before = now

    for copy in first:
        copy.wait_send()
    for k in range(levels):
        for i in range(east):
            scan_copy(k, i).wait_send()
    for i in range(east):
        copy_left(i).wait_send()
        copy_right(i).wait_send()
        copy_x(i).wait_send()
    zcopy.wait_send()


def shards(
    ngx,
    ngy,
    ngz,
    number_densities,
    kinetic_kelvin,
    flow_vector,
    opacity_area,
    illumination,
    arrhenius_coefficient,
    arrhenius_barrier,
    exothermic_energy,
    emission_loss,
    participant_indices,
    demanding_patches,
):
    kinds, east, north, lanes = number_densities.shape
    photons = opacity_area.shape[0]
    reactions = participant_indices.shape[1]
    two = reactions - photons
    slots = demanding_patches.shape[-1]
    patches = east * north
    levels = ngy.bit_length() - 1
    assert ngx == 2 and ngz == 2 and ngy == 1 << levels
    sizes = (kinds, east, north, lanes, photons, reactions, slots, ngy, levels)
    extents = (float(east * ngx), float(north * ngy), float(lanes * ngz))
    vmem = pl.BlockSpec(memory_space=pltpu.VMEM)
    smem = pl.BlockSpec(memory_space=pltpu.SMEM)
    tile = (kinds, lanes)
    DMA = pltpu.SemaphoreType.DMA
    out, warm = pl.pallas_call(
        functools.partial(kernel, sizes, extents),
        out_shape=(
            jax.ShapeDtypeStruct((kinds * patches, lanes), F32),
            jax.ShapeDtypeStruct((patches, lanes), F32),
        ),
        in_specs=[vmem] * 9 + [smem] * 2,
        out_specs=(vmem, vmem),
        scratch_shapes=[
            pltpu.VMEM((patches,) + tile, F32),
            pltpu.VMEM((patches, photons, lanes), F32),
            pltpu.VMEM((patches, photons, lanes), F32),
            pltpu.VMEM((patches,) + tile, F32),
            pltpu.VMEM((patches,) + tile, F32),
            pltpu.VMEM((north,) + tile, F32),
            pltpu.VMEM((north,) + tile, F32),
            pltpu.VMEM(tile, F32),
            pltpu.VMEM(tile, F32),
            pltpu.VMEM((levels + 1, east) + tile, F32),
            pltpu.VMEM((levels, east) + tile, F32),
            pltpu.VMEM((east,) + tile, F32),
            pltpu.VMEM((patches, lanes), F32),
            pltpu.VMEM((patches, lanes), F32),
            pltpu.VMEM((patches, lanes), F32),
            pltpu.VMEM((patches, lanes), F32),
            pltpu.VMEM((patches,) + tile, F32),
            pltpu.VMEM((2 * east,) + tile, F32),
            pltpu.VMEM((2 * east,) + tile, F32),
            pltpu.VMEM(tile, F32),
            pltpu.VMEM(tile, F32),
            pltpu.VMEM((slots,) + tile, F32),
            pltpu.VMEM((8, lanes), F32),
            pltpu.VMEM((photons, 2 * kinds), BF16),
            pltpu.VMEM((photons, 2 * kinds), BF16),
            pltpu.VMEM((photons, lanes), F32),
            pltpu.VMEM((reactions + two + 16, 2 * kinds), BF16),
            pltpu.VMEM((2 * kinds + 16, reactions), BF16),
            pltpu.VMEM((2 * lanes, 2 * lanes), BF16),
            pltpu.VMEM((two, lanes), F32),
            pltpu.VMEM((two, lanes), F32),
            DMA((6,)),
            DMA((6,)),
            DMA((levels, east)),
            DMA((levels, east)),
            DMA((east,)),
            DMA((east,)),
            DMA((east,)),
            DMA((east,)),
            DMA((east,)),
            DMA((east,)),
            DMA((1,)),
            DMA((1,)),
        ],
        compiler_params=pltpu.CompilerParams(
            collective_id=0, has_side_effects=True, vmem_limit_bytes=48 << 20
        ),
    )(
        number_densities.reshape(kinds * patches, lanes),
        kinetic_kelvin.reshape(patches, lanes),
        flow_vector.reshape(3 * patches, lanes),
        jnp.concatenate([opacity_area, opacity_area], axis=1),
        arrhenius_coefficient.reshape(1, two),
        arrhenius_barrier.reshape(1, two),
        exothermic_energy.reshape(1, reactions),
        jnp.concatenate([emission_loss, emission_loss]).reshape(1, 2 * kinds),
        participant_indices,
        illumination,
        demanding_patches.reshape(slots),
    )
    return out.reshape(number_densities.shape), warm.reshape(kinetic_kelvin.shape)


def solution(mesh):
    cells = P(None, "gx", "gy", "gz")
    return jax.shard_map(
        functools.partial(shards, mesh.shape["gx"], mesh.shape["gy"], mesh.shape["gz"]),
        mesh=mesh,
        in_specs=(
            cells,
            P("gx", "gy", "gz"),
            cells,
            P(),
            P(),
            P(),
            P(),
            P(),
            P(),
            P(),
            P("gx", "gy", "gz", None),
        ),
        out_specs=(cells, P("gx", "gy", "gz")),
        check_vma=False,
    )
```

profile of v0, /device:TPU:0, one launch (start us, length us, event | category | flops | bytes accessed | tf_op | source)
XLA Modules:
  0.0 39.1 jit_solution(10755210105191825465)
XLA Ops:
  0.6 0.0 copy-start.9
  0.6 0.6 %copy-done.9 = f32[64]{0:T(128)S(1)} copy-done((f32[64]{0:T(128)S(1)}, f32[64]{0:T(128)}, u32[]{:S(2)}) %copy-start.9) | copy-done | bytes 280
  1.3 0.1 maximum_bitcast_fusion.emission_ref
  1.4 0.8 %copy.13 = f32[128,64]{1,0:T(8,128)S(1)} copy(f32[128,64]{0,1:T(8,128)} %param.14) | data formatting | bytes 65536 | tf_op args[3]
  2.2 0.0 copy-start.1
  2.2 0.0 copy-start.2
  2.2 0.0 copy-start.3
  2.2 0.0 copy-start.4
  2.3 0.0 copy-start.5
  2.3 0.0 copy-start.6
  2.3 0.0 copy-start.7
  2.3 0.0 copy-start.8
  2.3 0.1 pad_maximum_fusion.opacity_ref
  2.4 0.6 %copy-done.1 = f32[3,4,4,128]{3,2,1,0:T(4,128)S(1)} copy-done((f32[3,4,4,128]{3,2,1,0:T(4,128)S(1)}, f32[3,4,4,128]{3,2,1,0:T(4,128)}, u32[]{:S(2)}) %copy-start.1) | copy-done | bytes 24600
  3.0 0.0 copy-done.2
  3.0 0.0 copy-done.3
  3.0 0.0 copy-done.4
  3.0 0.0 copy-done.5
  3.0 0.0 copy-done.6
  3.0 0.0 copy-done.7
  3.0 0.0 copy-done.8
  3.0 0.0 copy-start
  3.0 1.0 %copy-done = f32[64,4,4,128]{3,2,1,0:T(4,128)S(1)} copy-done((f32[64,4,4,128]{3,2,1,0:T(4,128)S(1)}, f32[64,4,4,128]{3,2,1,0:T(4,128)}, u32[]{:S(2)}) %copy-start) | copy-done | bytes 524312
  4.0 33.6 %shard_map.122 = (f32[1024,128]{1,0:T(8,128)S(1)}, f32[16,128]{1,0:T(8,128)S(1)}) custom-call(f32[1024,128]{1,0:T(8,128)S(1)} %bitcast.11, f32[16,128]{1,0:T(8,128)S(1)} %bitcast.14, f32[48,128]{1,0:T(8,128)S(1)} %bitcast.13, f32[128,128]{1,0:T(8,128)S(1)} %pad_maximum_fusion.opacity_ref, f32[1,128]{1,0:T(1,128)S(1)} %bitcast.17, f32[1,128]{1,0:T(1,128)S(1)} %bitcast.18, ...), custom_call_target="tpu_custom_call" | custom-call | tf_op jit(solution)/shard_map/pallas_call | solution.py:537
  37.7 0.8 %copy.17 = f32[64,4,4,128]{3,2,1,0:T(4,128)} copy(f32[64,4,4,128]{3,2,1,0:T(4,128)S(1)} %bitcast.12) | data formatting | bytes 1048576
  38.5 0.6 %copy.18 = f32[4,4,128]{2,1,0:T(4,128)} copy(f32[4,4,128]{2,1,0:T(4,128)S(1)} %bitcast.15) | data formatting | bytes 16384
Async XLA Ops:
  0.6 0.7 %copy-start.9 = (f32[64]{0:T(128)S(1)}, f32[64]{0:T(128)}, u32[]{:S(2)}) copy-start(f32[64]{0:T(128)} %param.19) | copy-start | bytes 772
  2.2 0.7 %copy-start.1 = (f32[3,4,4,128]{3,2,1,0:T(4,128)S(1)}, f32[3,4,4,128]{3,2,1,0:T(4,128)}, u32[]{:S(2)}) copy-start(f32[3,4,4,128]{3,2,1,0:T(4,128)} %param.13) | copy-start | bytes 73732
  2.2 0.7 %copy-start.2 = (f32[4,4,128]{2,1,0:T(4,128)S(1)}, f32[4,4,128]{2,1,0:T(4,128)}, u32[]{:S(2)}) copy-start(f32[4,4,128]{2,1,0:T(4,128)} %param.12) | copy-start | bytes 24580
  2.2 0.7 %copy-start.3 = (s32[4,256]{1,0:T(4,128)S(1)}, s32[4,256]{1,0:T(4,128)}, u32[]{:S(2)}) copy-start(s32[4,256]{1,0:T(4,128)} %part_ref.1) | copy-start | bytes 12292
  2.2 0.7 %copy-start.4 = (f32[256]{0:T(256)S(1)}, f32[256]{0:T(256)}, u32[]{:S(2)}) copy-start(f32[256]{0:T(256)} %param.18) | copy-start | bytes 3076
  2.3 0.7 %copy-start.5 = (f32[128]{0:T(128)S(1)}, f32[128]{0:T(128)}, u32[]{:S(2)}) copy-start(f32[128]{0:T(128)} %param.16) | copy-start | bytes 1540
  2.3 0.7 %copy-start.6 = (f32[128]{0:T(128)S(1)}, f32[128]{0:T(128)}, u32[]{:S(2)}) copy-start(f32[128]{0:T(128)} %param.17) | copy-start | bytes 1540
  2.3 0.7 %copy-start.7 = (f32[6]{0:T(128)S(1)}, f32[6]{0:T(128)}, u32[]{:S(2)}) copy-start(f32[6]{0:T(128)} %illum_ref.1) | copy-start | bytes 76
  2.3 0.7 %copy-start.8 = (s32[1,1,1,4]{3,2,1,0:T(1,128)S(1)}, s32[1,1,1,4]{3,2,1,0:T(1,128)}, u32[]{:S(2)}) copy-start(s32[1,1,1,4]{3,2,1,0:T(1,128)} %param.21) | copy-start | bytes 52
  3.0 1.0 %copy-start = (f32[64,4,4,128]{3,2,1,0:T(4,128)S(1)}, f32[64,4,4,128]{3,2,1,0:T(4,128)}, u32[]{:S(2)}) copy-start(f32[64,4,4,128]{3,2,1,0:T(4,128)} %param.11) | copy-start | bytes 1572868
where the time goes:
time: 39.4 us; the launch traced here: 39.1 us
  Pallas kernels  33.6 us (85%)
  local copies, waits for them, and re-layouts  4.53 us (11%)
  between operations  0.76 us (2%)
    pallas_call x1, Pallas kernels, shards(): pl.pallas_call(functools.partial(kernel, sizes, extents), out_shape=(jax....  33.6 us
    unnamed x23, local copies, waits for them, and re-layouts  4.53 us

commit v1 on v0

--- a/solution.py
+++ b/solution.py
@@ -31,7 +31,7 @@
 def kernel(
     sizes,
     extents,
-    n_ref,
+    n_any,
     t_ref,
     flow_ref,
     opacity_ref,
@@ -44,6 +44,7 @@
     patch_ref,
     out_ref,
     warm_ref,
+    n_ref,
     tiles,
     depth,
     photo,
@@ -56,6 +57,12 @@
     scan,
     scan_in,
     below,
+    above,
+    ey_low,
+    ey_up,
+    first_a,
+    first_pc,
+    first_cool,
     flow_x,
     flow_l,
     flow_r,
@@ -71,10 +78,12 @@
     op_lo,
     pick,
     gather_mat,
-    tally_mat,
+    tally_p,
+    tally_t,
     tri,
     coef_b,
     barr_b,
+    sem_n,
     sem_first_s,
     sem_first_r,
     sem_scan_s,
@@ -99,7 +108,7 @@
     partners = [(gx, gy + (1 << k) * (1 - 2 * bits[k]), gz) for k in range(levels)]
 
     entry = pltpu.get_barrier_semaphore()
-    peers = [peer_x, peer_z, left, right] + partners
+    peers = [peer_x, peer_z] + partners
     for peer in peers:
         pl.semaphore_signal(entry, inc=1, device_id=peer, device_id_type=MESH)
 
@@ -115,6 +124,55 @@
 
     lane = lax.broadcasted_iota(jnp.int32, (kinds, lanes), 1)
 
+    n_copy = pltpu.make_async_copy(n_any, n_ref, sem_n.at[0])
+    n_copy.start()
+
+    op = opacity_ref[...].T
+    op = jnp.concatenate([op, op], axis=1)
+    op_high, op_low = halves(op)
+    op_hi[...] = op_high
+    lane_p = lax.broadcasted_iota(jnp.int32, op.shape, 1)
+    op_lo[...] = jnp.where(lane_p < kinds, op_low.astype(F32), 0.0).astype(BF16)
+
+    twice = lax.broadcasted_iota(jnp.int32, (2 * kinds, reactions), 0)
+    twice = jnp.where(twice >= kinds, twice - kinds, twice)
+    hot_a = (twice == part_ref[0:1, :]).astype(F32)
+    gather_mat[0:reactions, :] = hot_a.T.astype(BF16)
+    two = reactions - photons
+    hot_b = (twice[:, photons:] == part_ref[1:2, photons:]).astype(F32)
+    gather_mat[reactions : reactions + two, :] = hot_b.T.astype(BF16)
+    extra = lax.broadcasted_iota(jnp.int32, (16, 2 * kinds), 0)
+    q_high, q_low = halves(emission_ref[...])
+    gather_mat[reactions + two :, :] = jnp.where(
+        extra == 0, q_high.astype(F32), jnp.where(extra == 1, q_low.astype(F32), 0.0)
+    ).astype(BF16)
+
+    species = lax.broadcasted_iota(jnp.int32, (kinds, reactions), 0)
+    which = lax.broadcasted_iota(jnp.int32, (kinds, reactions), 1)
+    made = (species == part_ref[2:3, :]).astype(F32) + (species == part_ref[3:4, :]).astype(F32)
+    used_up = (species == part_ref[0:1, :]).astype(F32) + jnp.where(
+        which >= photons, (species == part_ref[1:2, :]).astype(F32), 0.0
+    )
+    extra = lax.broadcasted_iota(jnp.int32, (16, reactions), 0)
+    e_high, e_low = halves(energy_ref[...])
+    heats = jnp.where(
+        extra == 0, e_high.astype(F32), jnp.where(extra == 1, e_low.astype(F32), 0.0)
+    )
+    tally = jnp.concatenate([made, used_up, heats], axis=0)
+    tally_p[...] = jnp.concatenate([tally[:, :photons]] * 2, axis=1).astype(BF16)
+    tally_t[...] = jnp.concatenate([tally[:, photons:]] * 2, axis=1).astype(BF16)
+
+    source = lax.broadcasted_iota(jnp.int32, (2 * lanes, 2 * lanes), 0)
+    source = jnp.where(source >= lanes, source - lanes, source)
+    target = lax.broadcasted_iota(jnp.int32, (2 * lanes, 2 * lanes), 1)
+    tri[...] = jnp.where(
+        source < target, 1.0, jnp.where(source == target, 0.5, 0.0)
+    ).astype(BF16)
+
+    coef_b[...] = jnp.broadcast_to(coef_ref[...], (lanes, two)).T
+    barr_b[...] = jnp.broadcast_to(-barrier_ref[...], (lanes, two)).T
+
+    n_copy.wait()
     xs = [None] * north
     zt = jnp.zeros((kinds, lanes), F32)
     for i in range(east):
@@ -147,20 +205,6 @@
             flow_ref.at[pl.ds(0, patches)], flow_x, sem_first_s.at[2], sem_first_r.at[2], peer_x
         ),
         send(
-            flow_ref.at[pl.ds(patches, patches)],
-            flow_r,
-            sem_first_s.at[3],
-            sem_first_r.at[3],
-            left,
-        ),
-        send(
-            flow_ref.at[pl.ds(patches, patches)],
-            flow_l,
-            sem_first_s.at[4],
-            sem_first_r.at[4],
-            right,
-        ),
-        send(
             flow_ref.at[pl.ds(2 * patches, patches)],
             flow_z,
             sem_first_s.at[5],
@@ -171,50 +215,6 @@
     for copy in first:
         copy.start()
 
-    op = opacity_ref[...]
-    op_high, op_low = halves(op)
-    op_hi[...] = op_high
-    lane_p = lax.broadcasted_iota(jnp.int32, op.shape, 1)
-    op_lo[...] = jnp.where(lane_p < kinds, op_low.astype(F32), 0.0).astype(BF16)
-
-    twice = lax.broadcasted_iota(jnp.int32, (2 * kinds, reactions), 0)
-    twice = jnp.where(twice >= kinds, twice - kinds, twice)
-    hot_a = (twice == part_ref[0:1, :]).astype(F32)
-    gather_mat[0:reactions, :] = hot_a.T.astype(BF16)
-    two = reactions - photons
-    hot_b = (twice[:, photons:] == part_ref[1:2, photons:]).astype(F32)
-    gather_mat[reactions : reactions + two, :] = hot_b.T.astype(BF16)
-    extra = lax.broadcasted_iota(jnp.int32, (16, 2 * kinds), 0)
-    q_high, q_low = halves(emission_ref[...])
-    gather_mat[reactions + two :, :] = jnp.where(
-        extra == 0, q_high.astype(F32), jnp.where(extra == 1, q_low.astype(F32), 0.0)
-    ).astype(BF16)
-
-    species = lax.broadcasted_iota(jnp.int32, (kinds, reactions), 0)
-    which = lax.broadcasted_iota(jnp.int32, (kinds, reactions), 1)
-    tally_mat[0:kinds, :] = (
-        (species == part_ref[2:3, :]).astype(F32) + (species == part_ref[3:4, :]).astype(F32)
-    ).astype(BF16)
-    tally_mat[kinds : 2 * kinds, :] = (
-        (species == part_ref[0:1, :]).astype(F32)
-        + jnp.where(which >= photons, (species == part_ref[1:2, :]).astype(F32), 0.0)
-    ).astype(BF16)
-    extra = lax.broadcasted_iota(jnp.int32, (16, reactions), 0)
-    e_high, e_low = halves(energy_ref[...])
-    tally_mat[2 * kinds :, :] = jnp.where(
-        extra == 0, e_high.astype(F32), jnp.where(extra == 1, e_low.astype(F32), 0.0)
-    ).astype(BF16)
-
-    source = lax.broadcasted_iota(jnp.int32, (2 * lanes, 2 * lanes), 0)
-    source = jnp.where(source >= lanes, source - lanes, source)
-    target = lax.broadcasted_iota(jnp.int32, (2 * lanes, 2 * lanes), 1)
-    tri[...] = jnp.where(
-        source < target, 1.0, jnp.where(source == target, 0.5, 0.0)
-    ).astype(BF16)
-
-    coef_b[...] = jnp.broadcast_to(coef_ref[...], (lanes, two)).T
-    barr_b[...] = jnp.broadcast_to(-barrier_ref[...], (lanes, two)).T
-
     def project(x):
         s = stacked(x)
         return dot(op_hi[...], s) + dot(op_lo[...], s)
@@ -228,26 +228,34 @@
 
     lax.fori_loop(0, east, depth_row, 0)
 
-    def scan_level(k):
+    def scan_step(k, i):
         bit = bits[k].astype(F32)
-
-        def chunk(i, carry):
-            scan_copy(k, i).wait_recv()
-            got = scan_in[k, i]
+        scan_copy(k, i).wait_recv()
+        got = scan_in[k, i]
+        if k + 1 < levels:
             scan[k + 1, i] = scan[k, i] + got
-            if k == 0:
-                below[i] = bit * got
-            else:
-                below[i] = below[i] + bit * got
-            if k + 1 < levels:
-                scan_copy(k + 1, i).start()
-            return carry
-
-        lax.fori_loop(0, east, chunk, 0)
-
-    scan_level(0)
-
-    first[0].wait_recv()
+            scan_copy(k + 1, i).start()
+        if k == 0:
+            below[i] = bit * got
+            above[i] = (1.0 - bit) * got
+        else:
+            below[i] = below[i] + bit * got
+            above[i] = above[i] + (1.0 - bit) * got
+
+    def y_lines(i, carry):
+        ms = [depth[i * north + j] for j in range(north)]
+        whole = ms[0]
+        for m in ms[1:]:
+            whole = whole + m
+        run = None
+        for j in range(north):
+            low = 0.5 * ms[j] if run is None else run + 0.5 * ms[j]
+            t = i * north + j
+            ey_low[t] = illum_ref[2] * jnp.exp(low * (-1.0 / extents[1]))
+            ey_up[t] = illum_ref[3] * jnp.exp((whole - low) * (-1.0 / extents[1]))
+            run = ms[j] if run is None else run + ms[j]
+        return carry
+
     high_x = gx.astype(F32)
 
     def x_lines(j, carry):
@@ -266,99 +274,145 @@
             run = run + ms[i]
         return carry
 
-    lax.fori_loop(0, north, x_lines, 0)
-    if levels > 1:
-        scan_level(1)
-
-    first[1].wait_recv()
-    pick[...] = project(zother[...])
     high_z = gz.astype(F32)
-    lane_r = lax.broadcasted_iota(jnp.int32, (photons, lanes), 1)
-
-    def z_tile(t, carry):
-        high, low_part = halves(depth[t])
-        both = dot(jnp.concatenate([high, low_part], axis=1), tri[...])
-        other = jnp.sum(jnp.where(lane_r == t, pick[...], 0.0), axis=1, keepdims=True)
-        low = both[:, :lanes] + high_z * other
-        up = both[:, lanes:] + other - low
-        photo[t] = photo[t] + (
-            illum_ref[4] * jnp.exp(low * (-1.0 / extents[2]))
-            + illum_ref[5] * jnp.exp(up * (-1.0 / extents[2]))
-        )
-        return carry
-
-    lax.fori_loop(0, patches, z_tile, 0)
-    for k in range(2, levels):
-        scan_level(k)
-
-    def y_lines(i, carry):
-        run = project(below[i])
-        whole = project(scan[levels, i])
+
+    def z_row(i):
+        parts = []
+        for j in range(north):
+            high, low_part = halves(depth[i * north + j])
+            parts.append(jnp.concatenate([high, low_part], axis=1))
+        both = dot(jnp.concatenate(parts, axis=0), tri[...])
         for j in range(north):
             t = i * north + j
-            low = run + 0.5 * depth[t]
-            up = whole - low
+            other = pick[:, t : t + 1]
+            rows = slice(j * photons, (j + 1) * photons)
+            low = both[rows, :lanes] + high_z * other
+            up = both[rows, lanes:] + other - low
             photo[t] = photo[t] + (
-                illum_ref[2] * jnp.exp(low * (-1.0 / extents[1]))
-                + illum_ref[3] * jnp.exp(up * (-1.0 / extents[1]))
+                illum_ref[4] * jnp.exp(low * (-1.0 / extents[2]))
+                + illum_ref[5] * jnp.exp(up * (-1.0 / extents[2]))
             )
-            run = run + depth[t]
-        return carry
-
-    lax.fori_loop(0, east, y_lines, 0)
-
-    def react(ns, ts, ps, h):
-        count = len(ns)
+
+    def two_body(ns, ts):
         g = dot(gather_mat[...], jnp.concatenate([stacked(n) for n in ns], axis=1))
         rates = []
-        for q in range(count):
+        for q in range(len(ns)):
             c = slice(q * lanes, (q + 1) * lanes)
             speed = coef_b[...] * jnp.exp(barr_b[...] * (1.0 / ts[q]))
             rates.append(
-                halves(
-                    jnp.concatenate(
-                        [
-                            ps[q] * g[:photons, c],
-                            speed * g[photons:reactions, c] * g[reactions : reactions + two, c],
-                        ],
-                        axis=0,
-                    )
-                )
+                stacked(speed * g[photons:reactions, c] * g[reactions : reactions + two, c])
             )
-        pc = dot(tally_mat[...], jnp.concatenate([r[0] for r in rates], axis=1)) + dot(
-            tally_mat[...], jnp.concatenate([r[1] for r in rates], axis=1)
-        )
-        new_n, new_t = [], []
-        for q in range(count):
+        pc = dot(tally_t[...], jnp.concatenate(rates, axis=1))
+        result = []
+        for q in range(len(ns)):
             c = slice(q * lanes, (q + 1) * lanes)
-            n = ns[q]
-            gained, used = pc[:kinds, c], pc[kinds : 2 * kinds, c]
-            new_n.append((n + h * gained) * (n / (n + h * used)))
-            heat = pc[2 * kinds : 2 * kinds + 1, c] + pc[2 * kinds + 1 : 2 * kinds + 2, c]
             cool = (
                 g[reactions + two : reactions + two + 1, c]
                 + g[reactions + two + 1 : reactions + two + 2, c]
             )
-            new_t.append((ts[q] + h * heat) / (1.0 + h * cool))
+            result.append((g[:photons, c], pc[:, c], cool))
+        return result
+
+    def finish(ns, ts, ps, halfway, h):
+        rates = [stacked(p * half[0]) for p, half in zip(ps, halfway)]
+        pc_all = dot(tally_p[...], jnp.concatenate(rates, axis=1))
+        new_n, new_t = [], []
+        for q in range(len(ns)):
+            c = slice(q * lanes, (q + 1) * lanes)
+            n = ns[q]
+            pc = pc_all[:, c] + halfway[q][1]
+            gained, used = pc[:kinds], pc[kinds : 2 * kinds]
+            new_n.append((n + h * gained) * (n / (n + h * used)))
+            heat = pc[2 * kinds : 2 * kinds + 1] + pc[2 * kinds + 1 : 2 * kinds + 2]
+            new_t.append((ts[q] + h * heat) / (1.0 + h * halfway[q][2]))
         return new_n, new_t
+
+    def first_row(i, carry):
+        index = [i * north + j for j in range(north)]
+        found = two_body([tiles[t] for t in index], [t_ref[pl.ds(t, 1), :] for t in index])
+        for t, (a, pc, cool) in zip(index, found):
+            first_a[t] = a
+            first_pc[t] = pc
+            first_cool[pl.ds(t, 1), :] = cool
+        return carry
+
+    def x_part():
+        first[0].wait_recv()
+        lax.fori_loop(0, north, x_lines, 0)
+        first[1].wait_recv()
+        pick[...] = project(zother[...])
+
+    pieces = [
+        lambda: lax.fori_loop(0, east, y_lines, 0),
+        x_part,
+        lambda: lax.fori_loop(0, east, first_row, 0),
+    ] + [functools.partial(z_row, i) for i in range(east)]
+    stages = levels + east - 1
+    for stage in range(stages):
+        if stage < len(pieces):
+            pieces[stage]()
+        for k in range(levels - 1, -1, -1):
+            if 0 <= stage - k < east:
+                if stage == stages - 1 and k == levels - 1:
+                    for piece in pieces[stages:]:
+                        piece()
+                scan_step(k, stage - k)
+
+    flow_y = [
+        send(
+            flow_ref.at[pl.ds(patches, patches)],
+            flow_r,
+            sem_first_s.at[3],
+            sem_first_r.at[3],
+            left,
+        ),
+        send(
+            flow_ref.at[pl.ds(patches, patches)],
+            flow_l,
+            sem_first_s.at[4],
+            sem_first_r.at[4],
+            right,
+        ),
+    ]
+    for copy in flow_y:
+        copy.start()
+
+    def y_join(i, carry):
+        low = jnp.exp(project(below[i]) * (-1.0 / extents[1]))
+        up = jnp.exp(project(above[i]) * (-1.0 / extents[1]))
+        for j in range(north):
+            t = i * north + j
+            photo[t] = photo[t] + (ey_low[t] * low + ey_up[t] * up)
+        return carry
+
+    lax.fori_loop(0, east, y_join, 0)
 
     listed = [patch_ref[d] for d in range(slots)]
     chosen = [jnp.minimum(d, patches - 1) for d in listed]
-    for d in range(slots):
-        hard_n[d] = tiles[chosen[d]]
-        hard_t[pl.ds(d, 1), :] = t_ref[pl.ds(chosen[d], 1), :]
+    hard_p = lambda: [photo[chosen[d]] for d in range(slots)]
+
+    def keep(ns, ts):
+        for d in range(slots):
+            hard_n[d] = ns[d]
+            hard_t[pl.ds(d, 1), :] = ts[d]
+
+    keep(
+        *finish(
+            [tiles[t] for t in chosen],
+            [t_ref[pl.ds(t, 1), :] for t in chosen],
+            hard_p(),
+            [(first_a[t], first_pc[t], first_cool[pl.ds(t, 1), :]) for t in chosen],
+            1.0 / NSUB,
+        )
+    )
 
     def substep(_, carry):
         ns = [hard_n[d] for d in range(slots)]
         ts = [hard_t[pl.ds(d, 1), :] for d in range(slots)]
-        ps = [photo[chosen[d]] for d in range(slots)]
-        ns, ts = react(ns, ts, ps, 1.0 / NSUB)
-        for d in range(slots):
-            hard_n[d] = ns[d]
-            hard_t[pl.ds(d, 1), :] = ts[d]
-        return carry
-
-    lax.fori_loop(0, NSUB, substep, 0)
+        keep(*finish(ns, ts, hard_p(), two_body(ns, ts), 1.0 / NSUB))
+        return carry
+
+    lax.fori_loop(1, NSUB, substep, 0)
 
     def copy_left(i):
         return send(
@@ -392,7 +446,8 @@
         ns = [tiles[t] for t in index]
         ts = [t_ref[pl.ds(t, 1), :] for t in index]
         ps = [photo[t] for t in index]
-        ns, ts = react(ns, ts, ps, 1.0)
+        halfway = [(first_a[t], first_pc[t], first_cool[pl.ds(t, 1), :]) for t in index]
+        ns, ts = finish(ns, ts, ps, halfway, 1.0)
         for j in range(north):
             t = index[j]
             n, warm = ns[j], ts[j]
@@ -420,7 +475,7 @@
     zcopy = send(zpack, halo_z, sem_z_s.at[0], sem_z_r.at[0], peer_z)
     zcopy.start()
 
-    for copy in first[2:]:
+    for copy in first[2:] + flow_y:
         copy.wait_recv()
 
     def flux(face, behind2, behind, ahead, ahead2):
@@ -492,7 +547,7 @@
                 out_ref[pl.ds(t, kinds, stride=patches), :] = chem[t] - COURANT * change
             before = now
 
-    for copy in first:
+    for copy in first + flow_y:
         copy.wait_send()
     for k in range(levels):
         for i in range(east):
@@ -540,9 +595,10 @@
             jax.ShapeDtypeStruct((kinds * patches, lanes), F32),
             jax.ShapeDtypeStruct((patches, lanes), F32),
         ),
-        in_specs=[vmem] * 9 + [smem] * 2,
+        in_specs=[pl.BlockSpec(memory_space=pltpu.HBM)] + [vmem] * 8 + [smem] * 2,
         out_specs=(vmem, vmem),
         scratch_shapes=[
+            pltpu.VMEM((kinds * patches, lanes), F32),
             pltpu.VMEM((patches,) + tile, F32),
             pltpu.VMEM((patches, photons, lanes), F32),
             pltpu.VMEM((patches, photons, lanes), F32),
@@ -555,6 +611,12 @@
             pltpu.VMEM((levels + 1, east) + tile, F32),
             pltpu.VMEM((levels, east) + tile, F32),
             pltpu.VMEM((east,) + tile, F32),
+            pltpu.VMEM((east,) + tile, F32),
+            pltpu.VMEM((patches, photons, lanes), F32),
+            pltpu.VMEM((patches, photons, lanes), F32),
+            pltpu.VMEM((patches, photons, lanes), F32),
+            pltpu.VMEM((patches, 2 * kinds + 16, lanes), F32),
+            pltpu.VMEM((patches, lanes), F32),
             pltpu.VMEM((patches, lanes), F32),
             pltpu.VMEM((patches, lanes), F32),
             pltpu.VMEM((patches, lanes), F32),
@@ -570,10 +632,12 @@
             pltpu.VMEM((photons, 2 * kinds), BF16),
             pltpu.VMEM((photons, lanes), F32),
             pltpu.VMEM((reactions + two + 16, 2 * kinds), BF16),
-            pltpu.VMEM((2 * kinds + 16, reactions), BF16),
+            pltpu.VMEM((2 * kinds + 16, 2 * photons), BF16),
+            pltpu.VMEM((2 * kinds + 16, 2 * two), BF16),
             pltpu.VMEM((2 * lanes, 2 * lanes), BF16),
             pltpu.VMEM((two, lanes), F32),
             pltpu.VMEM((two, lanes), F32),
+            DMA((1,)),
             DMA((6,)),
             DMA((6,)),
             DMA((levels, east)),
@@ -594,7 +658,7 @@
         number_densities.reshape(kinds * patches, lanes),
         kinetic_kelvin.reshape(patches, lanes),
         flow_vector.reshape(3 * patches, lanes),
-        jnp.concatenate([opacity_area, opacity_area], axis=1),
+        opacity_area.T,
         arrhenius_coefficient.reshape(1, two),
         arrhenius_barrier.reshape(1, two),
         exothermic_energy.reshape(1, reactions),

time: 39.4 us -> 45.5 us (1.15)
  Pallas kernels: 33.6 us -> 39.2 us
  local copies, waits for them, and re-layouts: 4.53 us -> 5.13 us
    pallas_call x1, Pallas kernels: 33.6 us -> 39.2 us  [shards(): pl.pallas_call(functools.partial(kernel, sizes, extents), out_shape=(jax....]
    unnamed x23 -> x24, local copies, waits for them, and re-layouts: 4.53 us -> 5.13 us
where the time goes in v1:
time: 45.5 us; the launch traced here: 45.1 us
  Pallas kernels  39.2 us (86%)
  local copies, waits for them, and re-layouts  5.13 us (11%)
  between operations  0.71 us (2%)
    pallas_call x1, Pallas kernels, shards(): pl.pallas_call(functools.partial(kernel, sizes, extents), out_shape=(jax....  39.2 us
    unnamed x24, local copies, waits for them, and re-layouts  5.13 us

profile of v1, /device:TPU:0, one launch (start us, length us, event | category | flops | bytes accessed | tf_op | source)
XLA Modules:
  0.0 45.1 jit_solution(6783079469630266814)
XLA Ops:
  0.6 0.0 copy-start.10
  0.6 0.0 copy-start.3
  0.7 0.0 copy-start.4
  0.7 0.0 copy-start.7
  0.7 0.0 copy-start.8
  0.7 0.0 copy-start.9
  0.7 0.6 %copy-done.10 = f32[64]{0:T(128)S(1)} copy-done((f32[64]{0:T(128)S(1)}, f32[64]{0:T(128)}, u32[]{:S(2)}) %copy-start.10) | copy-done | bytes 280
  1.3 0.0 copy-start.5
  1.3 0.0 copy-start.6
  1.3 0.1 maximum_bitcast_fusion.emission_ref
  1.4 0.0 copy-done.3
  1.4 0.0 copy-done.4
  1.4 0.0 copy-done.7
  1.4 0.0 copy-done.8
  1.4 0.0 copy-done.9
  1.4 0.6 %copy-done.5 = f32[256]{0:T(256)S(1)} copy-done((f32[256]{0:T(256)S(1)}, f32[256]{0:T(256)}, u32[]{:S(2)}) %copy-start.5) | copy-done | bytes 1048
  2.0 0.0 copy-done.6
  2.0 0.0 copy-start
  2.0 1.0 %copy-done = f32[64,4,4,128]{3,2,1,0:T(4,128)S(1)} copy-done((f32[64,4,4,128]{3,2,1,0:T(4,128)S(1)}, f32[64,4,4,128]{3,2,1,0:T(4,128)}, u32[]{:S(2)}) %copy-start) | copy-done | bytes 524312
  3.0 0.0 copy-start.1
  3.0 0.8 %copy-done.1 = f32[128,64]{0,1:T(8,128)S(1)} copy-done((f32[128,64]{0,1:T(8,128)S(1)}, f32[128,64]{0,1:T(8,128)}, u32[]{:S(2)}) %copy-start.1) | copy-done | bytes 32792
  3.8 0.0 copy-start.2
  3.8 0.7 %copy-done.2 = f32[3,4,4,128]{3,2,1,0:T(4,128)S(1)} copy-done((f32[3,4,4,128]{3,2,1,0:T(4,128)S(1)}, f32[3,4,4,128]{3,2,1,0:T(4,128)}, u32[]{:S(2)}) %copy-start.2) | copy-done | bytes 24600
  4.5 39.2 %shard_map.122 = (f32[1024,128]{1,0:T(8,128)S(1)}, f32[16,128]{1,0:T(8,128)S(1)}) custom-call(f32[1024,128]{1,0:T(8,128)S(1)} %bitcast.12, f32[16,128]{1,0:T(8,128)S(1)} %bitcast.16, f32[48,128]{1,0:T(8,128)S(1)} %bitcast.15, f32[64,128]{1,0:T(8,128)S(1)} %bitcast.14, f32[1,128]{1,0:T(1,128)S(1)} %bitcast.19, f32[1,128]{1,0:T(1,128)S(1)} %bitcast.20, ...), custom_call_target="tpu_custom_call" | custom-call | tf_op jit(solution)/shard_map/pallas_call | solution.py:592
  43.7 0.8 %copy.15 = f32[64,4,4,128]{3,2,1,0:T(4,128)} copy(f32[64,4,4,128]{3,2,1,0:T(4,128)S(1)} %bitcast.13) | data formatting | bytes 1048576
  44.5 0.6 %copy.16 = f32[4,4,128]{2,1,0:T(4,128)} copy(f32[4,4,128]{2,1,0:T(4,128)S(1)} %bitcast.17) | data formatting | bytes 16384
Async XLA Ops:
  0.6 0.7 %copy-start.10 = (f32[64]{0:T(128)S(1)}, f32[64]{0:T(128)}, u32[]{:S(2)}) copy-start(f32[64]{0:T(128)} %param.19) | copy-start | bytes 772
  0.6 0.7 %copy-start.3 = (f32[4,4,128]{2,1,0:T(4,128)S(1)}, f32[4,4,128]{2,1,0:T(4,128)}, u32[]{:S(2)}) copy-start(f32[4,4,128]{2,1,0:T(4,128)} %param.12) | copy-start | bytes 24580
  0.7 0.7 %copy-start.4 = (s32[4,256]{1,0:T(4,128)S(1)}, s32[4,256]{1,0:T(4,128)}, u32[]{:S(2)}) copy-start(s32[4,256]{1,0:T(4,128)} %part_ref.1) | copy-start | bytes 12292
  0.7 0.7 %copy-start.7 = (f32[128]{0:T(128)S(1)}, f32[128]{0:T(128)}, u32[]{:S(2)}) copy-start(f32[128]{0:T(128)} %param.17) | copy-start | bytes 1540
  0.7 0.7 %copy-start.8 = (f32[6]{0:T(128)S(1)}, f32[6]{0:T(128)}, u32[]{:S(2)}) copy-start(f32[6]{0:T(128)} %illum_ref.1) | copy-start | bytes 76
  0.7 0.7 %copy-start.9 = (s32[1,1,1,4]{3,2,1,0:T(1,128)S(1)}, s32[1,1,1,4]{3,2,1,0:T(1,128)}, u32[]{:S(2)}) copy-start(s32[1,1,1,4]{3,2,1,0:T(1,128)} %param.21) | copy-start | bytes 52
  1.3 0.7 %copy-start.5 = (f32[256]{0:T(256)S(1)}, f32[256]{0:T(256)}, u32[]{:S(2)}) copy-start(f32[256]{0:T(256)} %param.18) | copy-start | bytes 3076
  1.3 0.7 %copy-start.6 = (f32[128]{0:T(128)S(1)}, f32[128]{0:T(128)}, u32[]{:S(2)}) copy-start(f32[128]{0:T(128)} %param.16) | copy-start | bytes 1540
  2.0 1.0 %copy-start = (f32[64,4,4,128]{3,2,1,0:T(4,128)S(1)}, f32[64,4,4,128]{3,2,1,0:T(4,128)}, u32[]{:S(2)}) copy-start(f32[64,4,4,128]{3,2,1,0:T(4,128)} %param.11) | copy-start | bytes 1572868
  3.0 0.8 %copy-start.1 = (f32[128,64]{0,1:T(8,128)S(1)}, f32[128,64]{0,1:T(8,128)}, u32[]{:S(2)}) copy-start(f32[128,64]{0,1:T(8,128)} %param.14) | copy-start | bytes 98308
  3.8 0.7 %copy-start.2 = (f32[3,4,4,128]{3,2,1,0:T(4,128)S(1)}, f32[3,4,4,128]{3,2,1,0:T(4,128)}, u32[]{:S(2)}) copy-start(f32[3,4,4,128]{3,2,1,0:T(4,128)} %param.13) | copy-start | bytes 73732

commit v2 on v1

--- a/solution.py
+++ b/solution.py
@@ -31,7 +31,7 @@
 def kernel(
     sizes,
     extents,
-    n_any,
+    n_ref,
     t_ref,
     flow_ref,
     opacity_ref,
@@ -44,7 +44,6 @@
     patch_ref,
     out_ref,
     warm_ref,
-    n_ref,
     tiles,
     depth,
     photo,
@@ -83,7 +82,6 @@
     tri,
     coef_b,
     barr_b,
-    sem_n,
     sem_first_s,
     sem_first_r,
     sem_scan_s,
@@ -124,55 +122,7 @@
 
     lane = lax.broadcasted_iota(jnp.int32, (kinds, lanes), 1)
 
-    n_copy = pltpu.make_async_copy(n_any, n_ref, sem_n.at[0])
-    n_copy.start()
-
-    op = opacity_ref[...].T
-    op = jnp.concatenate([op, op], axis=1)
-    op_high, op_low = halves(op)
-    op_hi[...] = op_high
-    lane_p = lax.broadcasted_iota(jnp.int32, op.shape, 1)
-    op_lo[...] = jnp.where(lane_p < kinds, op_low.astype(F32), 0.0).astype(BF16)
-
-    twice = lax.broadcasted_iota(jnp.int32, (2 * kinds, reactions), 0)
-    twice = jnp.where(twice >= kinds, twice - kinds, twice)
-    hot_a = (twice == part_ref[0:1, :]).astype(F32)
-    gather_mat[0:reactions, :] = hot_a.T.astype(BF16)
-    two = reactions - photons
-    hot_b = (twice[:, photons:] == part_ref[1:2, photons:]).astype(F32)
-    gather_mat[reactions : reactions + two, :] = hot_b.T.astype(BF16)
-    extra = lax.broadcasted_iota(jnp.int32, (16, 2 * kinds), 0)
-    q_high, q_low = halves(emission_ref[...])
-    gather_mat[reactions + two :, :] = jnp.where(
-        extra == 0, q_high.astype(F32), jnp.where(extra == 1, q_low.astype(F32), 0.0)
-    ).astype(BF16)
-
-    species = lax.broadcasted_iota(jnp.int32, (kinds, reactions), 0)
-    which = lax.broadcasted_iota(jnp.int32, (kinds, reactions), 1)
-    made = (species == part_ref[2:3, :]).astype(F32) + (species == part_ref[3:4, :]).astype(F32)
-    used_up = (species == part_ref[0:1, :]).astype(F32) + jnp.where(
-        which >= photons, (species == part_ref[1:2, :]).astype(F32), 0.0
-    )
-    extra = lax.broadcasted_iota(jnp.int32, (16, reactions), 0)
-    e_high, e_low = halves(energy_ref[...])
-    heats = jnp.where(
-        extra == 0, e_high.astype(F32), jnp.where(extra == 1, e_low.astype(F32), 0.0)
-    )
-    tally = jnp.concatenate([made, used_up, heats], axis=0)
-    tally_p[...] = jnp.concatenate([tally[:, :photons]] * 2, axis=1).astype(BF16)
-    tally_t[...] = jnp.concatenate([tally[:, photons:]] * 2, axis=1).astype(BF16)
-
-    source = lax.broadcasted_iota(jnp.int32, (2 * lanes, 2 * lanes), 0)
-    source = jnp.where(source >= lanes, source - lanes, source)
-    target = lax.broadcasted_iota(jnp.int32, (2 * lanes, 2 * lanes), 1)
-    tri[...] = jnp.where(
-        source < target, 1.0, jnp.where(source == target, 0.5, 0.0)
-    ).astype(BF16)
-
-    coef_b[...] = jnp.broadcast_to(coef_ref[...], (lanes, two)).T
-    barr_b[...] = jnp.broadcast_to(-barrier_ref[...], (lanes, two)).T
-
-    n_copy.wait()
+
     xs = [None] * north
     zt = jnp.zeros((kinds, lanes), F32)
     for i in range(east):
@@ -215,6 +165,51 @@
     for copy in first:
         copy.start()
 
+    op = opacity_ref[...].T
+    op = jnp.concatenate([op, op], axis=1)
+    op_high, op_low = halves(op)
+    op_hi[...] = op_high
+    lane_p = lax.broadcasted_iota(jnp.int32, op.shape, 1)
+    op_lo[...] = jnp.where(lane_p < kinds, op_low.astype(F32), 0.0).astype(BF16)
+
+    twice = lax.broadcasted_iota(jnp.int32, (2 * kinds, reactions), 0)
+    twice = jnp.where(twice >= kinds, twice - kinds, twice)
+    hot_a = (twice == part_ref[0:1, :]).astype(F32)
+    gather_mat[0:reactions, :] = hot_a.T.astype(BF16)
+    two = reactions - photons
+    hot_b = (twice[:, photons:] == part_ref[1:2, photons:]).astype(F32)
+    gather_mat[reactions : reactions + two, :] = hot_b.T.astype(BF16)
+    extra = lax.broadcasted_iota(jnp.int32, (16, 2 * kinds), 0)
+    q_high, q_low = halves(emission_ref[...])
+    gather_mat[reactions + two :, :] = jnp.where(
+        extra == 0, q_high.astype(F32), jnp.where(extra == 1, q_low.astype(F32), 0.0)
+    ).astype(BF16)
+
+    species = lax.broadcasted_iota(jnp.int32, (kinds, reactions), 0)
+    which = lax.broadcasted_iota(jnp.int32, (kinds, reactions), 1)
+    made = (species == part_ref[2:3, :]).astype(F32) + (species == part_ref[3:4, :]).astype(F32)
+    used_up = (species == part_ref[0:1, :]).astype(F32) + jnp.where(
+        which >= photons, (species == part_ref[1:2, :]).astype(F32), 0.0
+    )
+    extra = lax.broadcasted_iota(jnp.int32, (16, reactions), 0)
+    e_high, e_low = halves(energy_ref[...])
+    heats = jnp.where(
+        extra == 0, e_high.astype(F32), jnp.where(extra == 1, e_low.astype(F32), 0.0)
+    )
+    tally = jnp.concatenate([made, used_up, heats], axis=0)
+    tally_p[...] = jnp.concatenate([tally[:, :photons]] * 2, axis=1).astype(BF16)
+    tally_t[...] = jnp.concatenate([tally[:, photons:]] * 2, axis=1).astype(BF16)
+
+    source = lax.broadcasted_iota(jnp.int32, (2 * lanes, 2 * lanes), 0)
+    source = jnp.where(source >= lanes, source - lanes, source)
+    target = lax.broadcasted_iota(jnp.int32, (2 * lanes, 2 * lanes), 1)
+    tri[...] = jnp.where(
+        source < target, 1.0, jnp.where(source == target, 0.5, 0.0)
+    ).astype(BF16)
+
+    coef_b[...] = jnp.broadcast_to(coef_ref[...], (lanes, two)).T
+    barr_b[...] = jnp.broadcast_to(-barrier_ref[...], (lanes, two)).T
+
     def project(x):
         s = stacked(x)
         return dot(op_hi[...], s) + dot(op_lo[...], s)
@@ -241,6 +236,10 @@
         else:
             below[i] = below[i] + bit * got
             above[i] = above[i] + (1.0 - bit) * got
+
+    def scan_chunk(k, i, carry):
+        scan_step(k, i)
+        return carry
 
     def y_lines(i, carry):
         ms = [depth[i * north + j] for j in range(north)]
@@ -342,21 +341,21 @@
         first[1].wait_recv()
         pick[...] = project(zother[...])
 
-    pieces = [
-        lambda: lax.fori_loop(0, east, y_lines, 0),
-        x_part,
-        lambda: lax.fori_loop(0, east, first_row, 0),
-    ] + [functools.partial(z_row, i) for i in range(east)]
-    stages = levels + east - 1
-    for stage in range(stages):
-        if stage < len(pieces):
-            pieces[stage]()
-        for k in range(levels - 1, -1, -1):
-            if 0 <= stage - k < east:
-                if stage == stages - 1 and k == levels - 1:
-                    for piece in pieces[stages:]:
-                        piece()
-                scan_step(k, stage - k)
+    def z_part():
+        for i in range(east):
+            z_row(i)
+
+    def y_part():
+        lax.fori_loop(0, east, y_lines, 0)
+
+    def first_part():
+        lax.fori_loop(0, east, first_row, 0)
+
+    pieces = [[y_part], [x_part], [first_part, z_part]]
+    for k in range(levels):
+        for piece in pieces[k] if k < len(pieces) else []:
+            piece()
+        lax.fori_loop(0, east, functools.partial(scan_chunk, k), 0)
 
     flow_y = [
         send(
@@ -595,10 +594,9 @@
             jax.ShapeDtypeStruct((kinds * patches, lanes), F32),
             jax.ShapeDtypeStruct((patches, lanes), F32),
         ),
-        in_specs=[pl.BlockSpec(memory_space=pltpu.HBM)] + [vmem] * 8 + [smem] * 2,
+        in_specs=[vmem] * 9 + [smem] * 2,
         out_specs=(vmem, vmem),
         scratch_shapes=[
-            pltpu.VMEM((kinds * patches, lanes), F32),
             pltpu.VMEM((patches,) + tile, F32),
             pltpu.VMEM((patches, photons, lanes), F32),
             pltpu.VMEM((patches, photons, lanes), F32),
@@ -637,7 +635,6 @@
             pltpu.VMEM((2 * lanes, 2 * lanes), BF16),
             pltpu.VMEM((two, lanes), F32),
             pltpu.VMEM((two, lanes), F32),
-            DMA((1,)),
             DMA((6,)),
             DMA((6,)),
             DMA((levels, east)),

time: 45.5 us -> 39.1 us (0.86)
  Pallas kernels: 39.2 us -> 32.8 us
    pallas_call x1, Pallas kernels: 39.2 us -> 32.8 us  [shards(): pl.pallas_call(functools.partial(kernel, sizes, extents), out_shape=(jax....]
where the time goes in v2:
time: 39.1 us; the launch traced here: 38.8 us
  Pallas kernels  32.8 us (84%)
  local copies, waits for them, and re-layouts  5.13 us (13%)
  between operations  0.71 us (2%)
    pallas_call x1, Pallas kernels, shards(): pl.pallas_call(functools.partial(kernel, sizes, extents), out_shape=(jax....  32.8 us
    unnamed x24, local copies, waits for them, and re-layouts  5.13 us

profile of v2, /device:TPU:0, one launch (start us, length us, event | category | flops | bytes accessed | tf_op | source)
XLA Modules:
  0.0 38.8 jit_solution(3103449563293591948)
XLA Ops:
  0.6 0.0 copy-start.10
  0.6 0.0 copy-start.3
  0.7 0.0 copy-start.4
  0.7 0.0 copy-start.7
  0.7 0.0 copy-start.8
  0.7 0.0 copy-start.9
  0.7 0.6 %copy-done.10 = f32[64]{0:T(128)S(1)} copy-done((f32[64]{0:T(128)S(1)}, f32[64]{0:T(128)}, u32[]{:S(2)}) %copy-start.10) | copy-done | bytes 280
  1.3 0.0 copy-start.5
  1.3 0.0 copy-start.6
  1.3 0.1 maximum_bitcast_fusion.emission_ref
  1.4 0.0 copy-done.3
  1.4 0.0 copy-done.4
  1.4 0.0 copy-done.7
  1.4 0.0 copy-done.8
  1.4 0.0 copy-done.9
  1.4 0.6 %copy-done.5 = f32[256]{0:T(256)S(1)} copy-done((f32[256]{0:T(256)S(1)}, f32[256]{0:T(256)}, u32[]{:S(2)}) %copy-start.5) | copy-done | bytes 1048
  2.0 0.0 copy-done.6
  2.0 0.0 copy-start
  2.0 1.0 %copy-done = f32[64,4,4,128]{3,2,1,0:T(4,128)S(1)} copy-done((f32[64,4,4,128]{3,2,1,0:T(4,128)S(1)}, f32[64,4,4,128]{3,2,1,0:T(4,128)}, u32[]{:S(2)}) %copy-start) | copy-done | bytes 524312
  3.0 0.0 copy-start.1
  3.0 0.8 %copy-done.1 = f32[128,64]{0,1:T(8,128)S(1)} copy-done((f32[128,64]{0,1:T(8,128)S(1)}, f32[128,64]{0,1:T(8,128)}, u32[]{:S(2)}) %copy-start.1) | copy-done | bytes 32792
  3.8 0.0 copy-start.2
  3.8 0.7 %copy-done.2 = f32[3,4,4,128]{3,2,1,0:T(4,128)S(1)} copy-done((f32[3,4,4,128]{3,2,1,0:T(4,128)S(1)}, f32[3,4,4,128]{3,2,1,0:T(4,128)}, u32[]{:S(2)}) %copy-start.2) | copy-done | bytes 24600
  4.5 32.8 %shard_map.122 = (f32[1024,128]{1,0:T(8,128)S(1)}, f32[16,128]{1,0:T(8,128)S(1)}) custom-call(f32[1024,128]{1,0:T(8,128)S(1)} %bitcast.12, f32[16,128]{1,0:T(8,128)S(1)} %bitcast.16, f32[48,128]{1,0:T(8,128)S(1)} %bitcast.15, f32[64,128]{1,0:T(8,128)S(1)} %bitcast.14, f32[1,128]{1,0:T(1,128)S(1)} %bitcast.19, f32[1,128]{1,0:T(1,128)S(1)} %bitcast.20, ...), custom_call_target="tpu_custom_call" | custom-call | tf_op jit(solution)/shard_map/pallas_call | solution.py:591
  37.4 0.8 %copy.15 = f32[64,4,4,128]{3,2,1,0:T(4,128)} copy(f32[64,4,4,128]{3,2,1,0:T(4,128)S(1)} %bitcast.13) | data formatting | bytes 1048576
  38.2 0.6 %copy.16 = f32[4,4,128]{2,1,0:T(4,128)} copy(f32[4,4,128]{2,1,0:T(4,128)S(1)} %bitcast.17) | data formatting | bytes 16384
Async XLA Ops:
  0.6 0.7 %copy-start.10 = (f32[64]{0:T(128)S(1)}, f32[64]{0:T(128)}, u32[]{:S(2)}) copy-start(f32[64]{0:T(128)} %param.19) | copy-start | bytes 772
  0.6 0.7 %copy-start.3 = (f32[4,4,128]{2,1,0:T(4,128)S(1)}, f32[4,4,128]{2,1,0:T(4,128)}, u32[]{:S(2)}) copy-start(f32[4,4,128]{2,1,0:T(4,128)} %param.12) | copy-start | bytes 24580
  0.7 0.7 %copy-start.4 = (s32[4,256]{1,0:T(4,128)S(1)}, s32[4,256]{1,0:T(4,128)}, u32[]{:S(2)}) copy-start(s32[4,256]{1,0:T(4,128)} %part_ref.1) | copy-start | bytes 12292
  0.7 0.7 %copy-start.7 = (f32[128]{0:T(128)S(1)}, f32[128]{0:T(128)}, u32[]{:S(2)}) copy-start(f32[128]{0:T(128)} %param.17) | copy-start | bytes 1540
  0.7 0.7 %copy-start.8 = (f32[6]{0:T(128)S(1)}, f32[6]{0:T(128)}, u32[]{:S(2)}) copy-start(f32[6]{0:T(128)} %illum_ref.1) | copy-start | bytes 76
  0.7 0.7 %copy-start.9 = (s32[1,1,1,4]{3,2,1,0:T(1,128)S(1)}, s32[1,1,1,4]{3,2,1,0:T(1,128)}, u32[]{:S(2)}) copy-start(s32[1,1,1,4]{3,2,1,0:T(1,128)} %param.21) | copy-start | bytes 52
  1.3 0.7 %copy-start.5 = (f32[256]{0:T(256)S(1)}, f32[256]{0:T(256)}, u32[]{:S(2)}) copy-start(f32[256]{0:T(256)} %param.18) | copy-start | bytes 3076
  1.3 0.7 %copy-start.6 = (f32[128]{0:T(128)S(1)}, f32[128]{0:T(128)}, u32[]{:S(2)}) copy-start(f32[128]{0:T(128)} %param.16) | copy-start | bytes 1540
  2.0 1.0 %copy-start = (f32[64,4,4,128]{3,2,1,0:T(4,128)S(1)}, f32[64,4,4,128]{3,2,1,0:T(4,128)}, u32[]{:S(2)}) copy-start(f32[64,4,4,128]{3,2,1,0:T(4,128)} %param.11) | copy-start | bytes 1572868
  3.0 0.8 %copy-start.1 = (f32[128,64]{0,1:T(8,128)S(1)}, f32[128,64]{0,1:T(8,128)}, u32[]{:S(2)}) copy-start(f32[128,64]{0,1:T(8,128)} %param.14) | copy-start | bytes 98308
  3.8 0.7 %copy-start.2 = (f32[3,4,4,128]{3,2,1,0:T(4,128)S(1)}, f32[3,4,4,128]{3,2,1,0:T(4,128)}, u32[]{:S(2)}) copy-start(f32[3,4,4,128]{3,2,1,0:T(4,128)} %param.13) | copy-start | bytes 73732
